TPU v7x, 32 devices: a whole 2x2x4 slice. The times are simulated.
32 devices in a mesh: req: 8 (over z, x), tp: 4 (over y, core).
Axes of the slice: x: 2, y: 2, z: 4, core: 2. Of those that a mesh axis runs over, the one named last changes fastest.
Arguments:
- hidden_in: bfloat16 [8, 1024, 2048], P('req', None, 'tp'), may hold values from -6 to 6
- ln_gain: float32 [2048], replicated, may hold values from 0.25 to 1.75
- ln_bias: float32 [2048], replicated, may hold values from -1.5 to 1.5
- w_qkv: bfloat16 [3, 2048, 2048], P(None, None, 'tp'), may hold values from -0.125 to 0.125
- b_qkv: float32 [3, 2048], P(None, 'tp'), may hold values from -1.5 to 1.5
- w_out: bfloat16 [2048, 2048], P('tp'), may hold values from -0.125 to 0.125
- b_out: float32 [2048], replicated, may hold values from -1.5 to 1.5
- alibi_slope: float32 [16], P('tp'), may hold values from 2.4414063e-05 to 0.1
- prefix_k: bfloat16 [2048, 2048], P('req', 'tp'), may hold values from -160 to 160
- prefix_v: bfloat16 [2048, 2048], P('req', 'tp'), may hold values from -6 to 6
- suffix_len: int32 [8], P('req'), may hold values from 64 to 1024, as said below
- group_of: int32 [8], P('req'), may hold values from 0 to 1
- block_of_device: int32 [8], P('req'), may hold values from 0 to 7, each once
Outputs:
- mixed: bfloat16 [8, 1024, 2048], P('req', None, 'tp')
- cache_k: bfloat16 [8, 1024, 2048], P('req', None, 'tp')
- cache_v: bfloat16 [8, 1024, 2048], P('req', None, 'tp')
Inputs may be any that keep to these rules, and one draw needn't show every extreme that they name: `suffix_len`: every request has at least 64 live slots; some request has exactly 1024.
All inputs are finite; a program needn't handle non-finite values.
Results may differ from a plain program's by a relative error of at most 0.011.
Values may be sent and summed in bfloat16 or wider, within the bound.
A program may use at most 384 MiB of HBM per device.

v0:
```python
import jax
import jax.numpy as jnp
from jax import lax
from jax.sharding import PartitionSpec as P

EPS = 1e-05
NEGATIVE = -1e30


def on_device(
    hidden_in,
    ln_gain,
    ln_bias,
    w_qkv,
    b_qkv,
    w_out,
    b_out,
    alibi_slope,
    prefix_k,
    prefix_v,
    suffix_len,
    group_of,
    block_of_device,
):
    local_rows = hidden_in[0]
    slots = local_rows.shape[0]
    width_dev = local_rows.shape[1]
    gathered = lax.all_gather(local_rows, "tp", axis=1, tiled=True)
    values32 = gathered.astype(jnp.float32)
    center = values32 - jnp.mean(values32, axis=1, keepdims=True)
    spread = jnp.mean(center * center, axis=1, keepdims=True)
    normed = (center / jnp.sqrt(spread + EPS) * ln_gain + ln_bias).astype(jnp.bfloat16)
    projected = (
        jnp.einsum("sd,cdh->csh", normed, w_qkv, preferred_element_type=jnp.float32)
        + b_qkv[:, None, :]
    )
    projected = projected.astype(jnp.bfloat16)
    query, keys, values = (projected[0], projected[1], projected[2])
    length = suffix_len[0]
    my_group = group_of[0]
    slot_ids = lax.iota(jnp.int32, slots)
    live = slot_ids < length
    keys_out = jnp.where(live[:, None], keys, jnp.zeros_like(keys))
    values_out = jnp.where(live[:, None], values, jnp.zeros_like(values))
    heads_dev = alibi_slope.shape[0]
    head_size = query.shape[1] // heads_dev
    attn_scale = 1.0 / jnp.sqrt(jnp.float32(head_size))
    query_heads = query.reshape(slots, heads_dev, head_size)
    block_tokens = prefix_k.shape[0]
    half_count = lax.axis_size("req") // 2
    prefix_total = half_count * block_tokens
    block_numbers = jnp.full((block_tokens,), block_of_device[0], jnp.int32)
    query_pos = (prefix_total + slot_ids).astype(jnp.float32)
    key_piece = lax.all_gather(prefix_k, "req", axis=0, tiled=True)
    value_piece = lax.all_gather(prefix_v, "req", axis=0, tiled=True)
    number_piece = lax.all_gather(block_numbers, "req", axis=0, tiled=True)
    count = key_piece.shape[0]
    offsets = lax.iota(jnp.int32, count) % block_tokens
    key_pos = (number_piece % half_count * block_tokens + offsets).astype(jnp.float32)
    fold_allowed = number_piece // half_count == my_group
    compute_old_max = jnp.full((heads_dev, slots), NEGATIVE, jnp.float32)
    compute_key_heads = key_piece.reshape(count, heads_dev, head_size)
    compute_value_heads = value_piece.reshape(count, heads_dev, head_size)
    compute_scores = (
        jnp.einsum(
            "shd,khd->hsk", query_heads, compute_key_heads, preferred_element_type=jnp.float32
        )
        * attn_scale
    )
    compute_scores = compute_scores - alibi_slope[:, None, None] * (
        query_pos[None, :, None] - key_pos[None, None, :]
    )
    compute_scores = jnp.where(fold_allowed[None, None, :], compute_scores, NEGATIVE)
    compute_new_max = jnp.maximum(compute_old_max, jnp.max(compute_scores, axis=2))
    compute_weights = jnp.where(
        fold_allowed[None, None, :], jnp.exp(compute_scores - compute_new_max[:, :, None]), 0.0
    )
    compute_new_sum = jnp.sum(compute_weights, axis=2)
    compute_new_acc = jnp.einsum(
        "hsk,khd->hsd",
        compute_weights.astype(jnp.bfloat16),
        compute_value_heads,
        preferred_element_type=jnp.float32,
    )
    key_heads = keys.reshape(slots, heads_dev, head_size)
    value_heads = values.reshape(slots, heads_dev, head_size)
    row_block = min(512, slots)
    pieces_out = []
    for row_start in range(0, slots, row_block):
        row_stop = min(slots, row_start + row_block)
        row_ids = slot_ids[row_start:row_stop]
        query_block = query_heads[row_start:row_stop]
        scores = (
            jnp.einsum("shd,khd->hsk", query_block, key_heads, preferred_element_type=jnp.float32)
            * attn_scale
        )
        scores = (
            scores
            - alibi_slope[:, None, None]
            * (row_ids[:, None] - slot_ids[None, :]).astype(jnp.float32)[None]
        )
        allowed = (slot_ids[None, :] <= row_ids[:, None]) & (slot_ids[None, :] < length)
        scores = jnp.where(allowed[None], scores, NEGATIVE)
        old_max = compute_new_max[:, row_start:row_stop]
        new_max = jnp.maximum(old_max, jnp.max(scores, axis=2))
        weights = jnp.where(allowed[None], jnp.exp(scores - new_max[:, :, None]), 0.0)
        factor = jnp.exp(old_max - new_max)
        new_sum = compute_new_sum[:, row_start:row_stop] * factor + jnp.sum(weights, axis=2)
        new_acc = compute_new_acc[:, row_start:row_stop] * factor[:, :, None] + jnp.einsum(
            "hsk,khd->hsd",
            weights.astype(jnp.bfloat16),
            value_heads,
            preferred_element_type=jnp.float32,
        )
        piece_out = new_acc / new_sum[:, :, None]
        pieces_out.append(piece_out)
    attended = jnp.concatenate(pieces_out, axis=1)
    attended = (
        attended.transpose(1, 0, 2).reshape(slots, heads_dev * head_size).astype(jnp.bfloat16)
    )
    partial_value = jnp.dot(attended, w_out, preferred_element_type=jnp.float32)
    summed = lax.psum_scatter(
        partial_value.astype(jnp.bfloat16), "tp", scatter_dimension=1, tiled=True
    ).astype(jnp.float32)
    bias_part = lax.dynamic_slice_in_dim(b_out, lax.axis_index("tp") * width_dev, width_dev)
    result = summed + bias_part + local_rows.astype(jnp.float32)
    result = jnp.where(live[:, None], result, 0.0).astype(jnp.bfloat16)
    return (result[None], keys_out[None], values_out[None])


def solution(mesh):
    return jax.shard_map(
        on_device,
        mesh=mesh,
        in_specs=(
            P("req", None, "tp"),
            P(),
            P(),
            P(None, None, "tp"),
            P(None, "tp"),
            P("tp", None),
            P(),
            P("tp"),
            P("req", "tp"),
            P("req", "tp"),
            P("req"),
            P("req"),
            P("req"),
        ),
        out_specs=(P("req", None, "tp"), P("req", None, "tp"), P("req", None, "tp")),
        check_vma=False,
    )
```

profile of v0, /device:TPU:0, one launch (start us, length us, event | category | flops | bytes accessed | tf_op | source)
XLA Modules:
  0.0 241.2 jit_solution(5262396388451075236)
XLA Ops:
  7.2 0.7 all-gather.10.cloned.1.call-update
  8.0 1.8 copy.42
  9.8 0.0 all-gather.8.cloned.1.call-start
  9.8 1.8 copy.45
  12.4 2.4 subtract_convert_fusion
  14.8 1.8 fusion.35
  17.2 22.2 %all-gather.1 = s32[8,1,256]{2,1,0:T(1,128)S(1)} all-gather(s32[1,1,256]{2,1,0:T(1,128)S(1)} %broadcast.168), channel_id=1, replica_groups=mesh['req'=8,'tp'=4] {'req'}, dimensions={0}, use_global_device_ids=true | all-gather | bytes 9216 | tf_op jit(solution)/shard_map/all_gather | solution.py:56
  40.2 3.8 %broadcast_subtract_fusion = f32[1024,2048]{1,0:T(8,128)} fusion(f32[2048]{0:T(1024)S(1)} %fusion.50, f32[1024]{0:T(1024)S(1)} %add_convert_fusion.1), kind=kLoop, calls=%fused_computation.28 | loop fusion | flops 2097152 | bytes 8400896 | tf_op jit(solution)/shard_map/sub | solution.py:71
  44.0 2.8 %all-gather.10.cloned.1.call-done = bf16[1,1024,2048]{2,1,0:T(8,128)(2,1)} async-done(((bf16[1,1024,512]{2,1,0:T(8,128)(2,1)}), bf16[1,1024,2048]{2,1,0:T(8,128)(2,1)}) %all-gather.10.cloned.1.call-update) | async-done | bytes 4194320 | tf_op jit(solution)/shard_map/all_gather | solution.py:28
  46.8 3.0 %convert_reduce_fusion = f32[1024]{0:T(1024)S(1)} fusion(bf16[1,1024,2048]{2,1,0:T(8,128)(2,1)} %all-gather.10.cloned.1.call-done), kind=kLoop, calls=%fused_computation.6 | loop fusion | flops 4193280 | bytes 4198400 | tf_op jit(solution)/shard_map/reduce_sum | solution.py:30
  49.8 3.4 %fusion.8 = f32[1024]{0:T(1024)S(1)} fusion(bf16[1,1024,2048]{2,1,0:T(8,128)(2,1)} %all-gather.10.cloned.1.call-done, f32[1024]{0:T(1024)S(1)} %broadcast_multiply_fusion), kind=kLoop, calls=%fused_computation.11 | loop fusion | flops 8387584 | bytes 4202496 | tf_op jit(solution)/shard_map/reduce_sum | solution.py:31
  53.2 11.3 %fusion.29 = bf16[3,1024,512]{1,2,0:T(8,128)(2,1)S(1)} fusion(f32[3,512]{1,0:T(4,128)S(1)} %copy-done.15, bf16[3,2048,512]{2,1,0:T(8,128)(2,1)} %param.16, bf16[1,1024,2048]{2,1,0:T(8,128)(2,1)S(1)} %copy-done.1, f32[2048]{0:T(1024)S(1)} %copy-done.16, f32[2048]{0:T(1024)S(1)} %copy-done.17, f32[1024]{0:T(1024)S(1)} %add_sqrt_fusion, ...), kind=kOutput, calls=%fused_computation.36 | convolution fusion | flops 6458179584 | bytes 13662208 | tf_op jit(solution)/shard_map/sd,cdh->csh/dot_general | solution.py:34
  64.5 2.1 broadcast_select_fusion
  66.7 1.1 fusion.65
  67.7 32.2 %all-gather.6.cloned.1.call-done = bf16[2048,512]{0,1:T(8,128)(2,1)} async-done(((bf16[256,512]{0,1:T(8,128)(2,1)}), bf16[2048,512]{0,1:T(8,128)(2,1)}) %all-gather.6.cloned.1.call-update) | async-done | bytes 2097168 | tf_op jit(solution)/shard_map/all_gather | solution.py:54
  99.9 17.8 %fusion.66 = (f32[4,1024]{1,0:T(4,128)S(1)}, f32[4,1024,2048]{2,1,0:T(8,128)}) fusion(f32[1024,2048]{1,0:T(8,128)} %broadcast_subtract_fusion, f32[4]{0:T(128)S(1)} %copy-done.14, bf16[1024,4,128]{0,2,1:T(8,128)(2,1)S(1)} %bitcast.62, bf16[2048,4,128]{0,2,1:T(8,128)(2,1)} %bitcast.63, pred[2048]{0:T(1024)(128)(4,1)S(1)} %fusion.47), kind=kOutput, calls=%fused_computation.94 | convolution fusion | flops 2189422592 | bytes 45107216 | tf_op jit(solution)/shard_map/shd,khd->hsk/dot_general | solution.py:65
  117.8 4.5 %fusion.16 = (f32[4,512]{1,0:T(4,128)S(1)}, f32[4,512,1024]{2,1,0:T(8,128)S(1)}) fusion(f32[512,1024]{1,0:T(8,128)} %get-tuple-element.35, f32[4]{0:T(128)S(1)} %copy-done.14, pred[512,1024]{1,0:T(8,128)(4,1)} %get-tuple-element.28, bf16[512,4,128]{0,2,1:T(8,128)(2,1)} %bitcast.70, bf16[1024,4,128]{0,2,1:T(8,128)(2,1)} %bitcast.66), kind=kOutput, calls=%fused_computation.24 | convolution fusion | flops 547354624 | bytes 12591120 | tf_op jit(solution)/shard_map/shd,khd->hsk/dot_general | solution.py:94
  122.4 7.8 %fusion.12 = (f32[4,512]{1,0:T(4,128)S(1)}, f32[4,512]{1,0:T(4,128)S(1)}, f32[4,512,1024]{2,1,0:T(8,128)}) fusion(f32[4,512,1024]{2,1,0:T(8,128)S(1)} %get-tuple-element.30, f32[4,512]{1,0:T(4,128)S(1)} %slice_maximum_fusion.1, f32[512,1024]{1,0:T(8,128)S(1)} %copy-done.7, f32[4]{0:T(128)S(1)} %copy-done.14, pred[512,1024]{1,0:T(8,128)(4,1)S(1)} %copy-done.11, ...), kind=kOutput, calls=%fused_computation.19 | convolution fusion | flops 562032640 | bytes 23617552 | tf_op jit(solution)/shard_map/shd,khd->hsk/dot_general | solution.py:94
  130.2 14.3 %fusion = f32[4,1024]{1,0:T(4,128)S(1)} fusion(f32[4,1024,2048]{2,1,0:T(8,128)} %get-tuple-element.32, f32[4,1024]{1,0:T(4,128)S(1)} %broadcast_maximum_fusion, pred[2048]{0:T(1024)(128)(4,1)S(1)} %fusion.47), kind=kLoop, calls=%fused_computation.2 | loop fusion | flops 25161728 | bytes 33589248 | tf_op jit(solution)/shard_map/reduce_sum | solution.py:78
  144.6 6.7 %all-gather.8.cloned.1.call-done = bf16[2048,512]{0,1:T(8,128)(2,1)} async-done(((bf16[256,512]{0,1:T(8,128)(2,1)}), bf16[2048,512]{0,1:T(8,128)(2,1)}) %all-gather.8.cloned.1.call-update) | async-done | bytes 2097168 | tf_op jit(solution)/shard_map/all_gather | solution.py:55
  151.3 15.1 %fusion.2 = f32[4,1024,128]{2,1,0:T(8,128)} fusion(bf16[2048,4,128]{0,2,1:T(8,128)(2,1)} %bitcast.73, f32[4,1024,2048]{2,1,0:T(8,128)} %get-tuple-element.32, f32[4,1024]{1,0:T(4,128)S(1)} %broadcast_maximum_fusion, pred[2048]{0:T(1024)(128)(4,1)S(1)} %fusion.47), kind=kOutput, calls=%fused_computation.4 | convolution fusion | flops 2172649472 | bytes 37767168 | tf_op jit(solution)/shard_map/hsk,khd->hsd/dot_general | solution.py:79
  166.4 6.0 %fusion.14 = f32[4,512]{1,0:T(4,128)S(1)} fusion(f32[4,512,1024]{2,1,0:T(8,128)} %get-tuple-element.33, f32[4,512]{1,0:T(4,128)S(1)} %slice_maximum_fusion, f32[512,1024]{1,0:T(8,128)S(1)} %copy-done.4, f32[4]{0:T(128)S(1)} %copy-done.14, pred[512,1024]{1,0:T(8,128)(4,1)S(1)} %copy-done.6), kind=kLoop, calls=%fused_computation.21 | loop fusion | flops 14678016 | bytes 11026448 | tf_op jit(solution)/shard_map/reduce_sum | solution.py:108
  172.5 5.8 %divide_convert_fusion = bf16[4,512,128]{2,1,0:T(8,128)(2,1)S(1)} fusion(bf16[1024,4,128]{0,2,1:T(8,128)(2,1)S(1)} %bitcast.64, f32[4,512,1024]{2,1,0:T(8,128)S(1)} %copy-done.2, f32[4,512]{1,0:T(4,128)S(1)} %slice_maximum_fusion, f32[512,1024]{1,0:T(8,128)S(1)} %copy-done.4, f32[4]{0:T(128)S(1)} %copy-done.14, pred[512,1024]{1,0:T(8,128)(4,1)S(1)} %copy-done.6, ...), kind=kOutput, calls=%fused_computation.52 | convolution fusion | flops 552599552 | bytes 13656080 | tf_op jit(solution)/shard_map/hsk,khd->hsd/dot_general | solution.py:109
  178.4 3.8 %divide_convert_fusion.1 = bf16[4,512,128]{2,1,0:T(8,128)(2,1)S(1)} fusion(bf16[1024,4,128]{0,2,1:T(8,128)(2,1)S(1)} %bitcast.65, f32[4,512,1024]{2,1,0:T(8,128)S(1)} %bitcast.75, f32[4,512]{1,0:T(4,128)S(1)} %slice_maximum_fusion.1, f32[512,1024]{1,0:T(8,128)S(1)} %copy-done.8, f32[4]{0:T(128)S(1)} %copy-done.14, pred[512,1024]{1,0:T(8,128)(4,1)S(1)} %copy-done.12, ...), kind=kOutput, calls=%fused_computation.53 | convolution fusion | flops 552599552 | bytes 13656080 | tf_op jit(solution)/shard_map/hsk,khd->hsd/dot_general | solution.py:109
  182.1 0.1 maximum_bitcast_fusion
  182.2 1.3 copy.53
  183.5 5.7 %convolution_convert_fusion = bf16[1024,2048]{1,0:T(8,128)(2,1)} fusion(bf16[1024,512]{0,1:T(8,128)(2,1)} %bitcast.68, bf16[512,2048]{1,0:T(8,128)(2,1)S(1)} %copy-done), kind=kOutput, calls=%fused_computation.35 | convolution fusion | flops 2149580800 | bytes 7340032 | tf_op jit(solution)/shard_map/dot_general | solution.py:121
  189.2 0.8 dynamic_slice.3
  190.0 2.3 copy.54
  192.3 2.5 %copy.55 = bf16[1,1024,512]{2,1,0:T(8,128)(2,1)} copy(bf16[1,1024,512]{1,2,0:T(8,128)(2,1)} %get-tuple-element.18) | data formatting | bytes 2097152
  194.8 37.3 %reduce-scatter.2.cloned.1.call-done = bf16[1024,512]{1,0:T(8,128)(2,1)} async-done(((bf16[1024,2048]{1,0:T(8,128)(2,1)}), bf16[1024,512]{1,0:T(8,128)(2,1)}) %reduce-scatter.2.cloned.1.call-update) | async-done | bytes 1048592 | tf_op jit(solution)/shard_map/reduce_scatter | solution.py:122
  232.1 2.6 %fusion.42 = bf16[1,1024,512]{2,1,0:T(8,128)(2,1)} fusion(bf16[1024,512]{1,0:T(8,128)(2,1)} %reduce-scatter.2.cloned.1.call-done, bf16[1,1024,512]{2,1,0:T(8,128)(2,1)S(1)} %copy-done.5, f32[512]{0:T(512)S(1)} %dynamic_slice.3, pred[1024]{0:T(1024)(128)(4,1)S(1)} %iota_compare_fusion.2), kind=kLoop, calls=%fused_computation.48 | loop fusion | flops 3145728 | bytes 3148800 | tf_op jit(solution)/shard_map/broadcast_in_dim | solution.py:128
  (66 shorter events, 0.4 us)
Async XLA Ops:
  7.2 176.4 %copy-start = (bf16[512,2048]{1,0:T(8,128)(2,1)S(1)}, bf16[512,2048]{1,0:T(8,128)(2,1)}, u32[]{:S(2)}) copy-start(bf16[512,2048]{1,0:T(8,128)(2,1)} %param.18) | copy-start | bytes 6291460
  7.2 39.6 %all-gather.10.cloned.1.call-start = ((), (), s32[]{:S(2)}) async-start(), calls=%async_computation.4 | async-start | bytes 5242880 | tf_op jit(solution)/shard_map/all_gather | solution.py:28
  7.9 92.0 %all-gather.6.cloned.1.call-start = ((), (), s32[]{:S(2)}) async-start(), calls=%async_computation.1 | async-start | bytes 2359296 | tf_op jit(solution)/shard_map/all_gather | solution.py:54
  9.8 141.5 %all-gather.8.cloned.1.call-start = ((), (), s32[]{:S(2)}) async-start(), calls=%async_computation.2 | async-start | bytes 2359296 | tf_op jit(solution)/shard_map/all_gather | solution.py:55
  11.6 220.5 %reduce-scatter.2.cloned.1.call-start = ((), (), s32[]{:S(2)}) async-start(), calls=%async_computation.3 | async-start | bytes 5242880 | tf_op jit(solution)/shard_map/reduce_scatter | solution.py:122
  40.2 13.0 %copy-start.15 = (f32[3,512]{1,0:T(4,128)S(1)}, f32[3,512]{1,0:T(4,128)}, u32[]{:S(2)}) copy-start(f32[3,512]{1,0:T(4,128)} %param.17) | copy-start | bytes 18436
  40.2 13.0 %copy-start.16 = (f32[2048]{0:T(1024)S(1)}, f32[2048]{0:T(1024)}, u32[]{:S(2)}) copy-start(f32[2048]{0:T(1024)} %param.15) | copy-start | bytes 24580
  40.2 13.0 %copy-start.17 = (f32[2048]{0:T(1024)S(1)}, f32[2048]{0:T(1024)}, u32[]{:S(2)}) copy-start(f32[2048]{0:T(1024)} %param.14) | copy-start | bytes 24580
  46.8 6.4 %copy-start.1 = (bf16[1,1024,2048]{2,1,0:T(8,128)(2,1)S(1)}, bf16[1,1024,2048]{2,1,0:T(8,128)(2,1)}, u32[]{:S(2)}) copy-start(bf16[1,1024,2048]{2,1,0:T(8,128)(2,1)} %all-gather.10.cloned.1.call-done) | copy-start | bytes 12582916
  64.5 35.4 %copy-start.14 = (f32[4]{0:T(128)S(1)}, f32[4]{0:T(128)}, u32[]{:S(2)}) copy-start(f32[4]{0:T(128)} %param.20) | copy-start | bytes 52
  117.8 4.6 %copy-start.3 = (f32[512,1024]{1,0:T(8,128)S(1)}, f32[512,1024]{1,0:T(8,128)}, u32[]{:S(2)}) copy-start(f32[512,1024]{1,0:T(8,128)} %get-tuple-element.34) | copy-start | bytes 6291460
  117.8 4.6 %copy-start.6 = (pred[512,1024]{1,0:T(8,128)(4,1)S(1)}, pred[512,1024]{1,0:T(8,128)(4,1)}, u32[]{:S(2)}) copy-start(pred[512,1024]{1,0:T(8,128)(4,1)} %get-tuple-element.27) | copy-start | bytes 1572868
  117.8 4.6 %copy-start.7 = (f32[512,1024]{1,0:T(8,128)S(1)}, f32[512,1024]{1,0:T(8,128)}, u32[]{:S(2)}) copy-start(f32[512,1024]{1,0:T(8,128)} %get-tuple-element.35) | copy-start | bytes 6291460
  117.8 4.6 %copy-start.10 = (bf16[1,1024,512]{1,2,0:T(8,128)(2,1)S(1)}, bf16[1,1024,512]{1,2,0:T(8,128)(2,1)}, u32[]{:S(2)}) copy-start(bf16[1,1024,512]{1,2,0:T(8,128)(2,1)} %get-tuple-element.21) | copy-start | bytes 3145732
  117.8 4.6 %copy-start.11 = (pred[512,1024]{1,0:T(8,128)(4,1)S(1)}, pred[512,1024]{1,0:T(8,128)(4,1)}, u32[]{:S(2)}) copy-start(pred[512,1024]{1,0:T(8,128)(4,1)} %get-tuple-element.28) | copy-start | bytes 1572868
  117.8 4.6 %copy-start.13 = (bf16[1,512,512]{1,2,0:T(8,128)(2,1)S(1)}, bf16[1,512,512]{1,2,0:T(8,128)(2,1)}, u32[]{:S(2)}) copy-start(bf16[1,512,512]{1,2,0:T(8,128)(2,1)} %get-tuple-element.24) | copy-start | bytes 1572868
  122.4 7.9 %copy-start.18 = (f32[4,512,1024]{2,1,0:T(8,128)}, f32[4,512,1024]{2,1,0:T(8,128)S(1)}, u32[]{:S(2)}) copy-start(f32[4,512,1024]{2,1,0:T(8,128)S(1)} %get-tuple-element.30) | copy-start | bytes 25165828
  151.3 15.1 %copy-start.4 = (f32[512,1024]{1,0:T(8,128)S(1)}, f32[512,1024]{1,0:T(8,128)}, u32[]{:S(2)}) copy-start(f32[512,1024]{1,0:T(8,128)} %get-tuple-element.34) | copy-start | bytes 6291460
  166.3 6.1 %copy-start.2 = (f32[4,512,1024]{2,1,0:T(8,128)S(1)}, f32[4,512,1024]{2,1,0:T(8,128)}, u32[]{:S(2)}) copy-start(f32[4,512,1024]{2,1,0:T(8,128)} %get-tuple-element.33) | copy-start | bytes 25165828
  166.4 6.1 %copy-start.9 = (bf16[1,1024,512]{1,2,0:T(8,128)(2,1)S(1)}, bf16[1,1024,512]{1,2,0:T(8,128)(2,1)}, u32[]{:S(2)}) copy-start(bf16[1,1024,512]{1,2,0:T(8,128)(2,1)} %get-tuple-element.20) | copy-start | bytes 3145732
  166.4 12.0 %slice-start = ((s8[8388608]{0:T(1024)(128)(4,1)}), s8[4194304]{0:T(1024)(128)(4,1)S(1)}, s32[]{:S(2)}) async-start(s8[8388608]{0:T(1024)(128)(4,1)} %bitcast.74), calls=%async_computation.5 | async-start | bytes 8388608
  172.4 5.9 %copy-start.8 = (f32[512,1024]{1,0:T(8,128)S(1)}, f32[512,1024]{1,0:T(8,128)}, u32[]{:S(2)}) copy-start(f32[512,1024]{1,0:T(8,128)} %get-tuple-element.35) | copy-start | bytes 6291460
  172.5 5.9 %copy-start.12 = (pred[512,1024]{1,0:T(8,128)(4,1)S(1)}, pred[512,1024]{1,0:T(8,128)(4,1)}, u32[]{:S(2)}) copy-start(pred[512,1024]{1,0:T(8,128)(4,1)} %get-tuple-element.28) | copy-start | bytes 1572868
  172.5 5.9 %slice-start.1 = ((s8[8388608]{0:T(1024)(128)(4,1)}), s8[4194304]{0:T(1024)(128)(4,1)S(1)}, s32[]{:S(2)}) async-start(s8[8388608]{0:T(1024)(128)(4,1)} %bitcast.74), calls=%async_computation.6 | async-start | bytes 8388608
  172.5 5.9 %copy-start.19 = (f32[4,1024,128]{2,1,0:T(8,128)S(1)}, f32[4,1024,128]{2,1,0:T(8,128)}, u32[]{:S(2)}) copy-start(f32[4,1024,128]{2,1,0:T(8,128)} %fusion.2) | copy-start | bytes 6291460
  183.5 48.6 %copy-start.5 = (bf16[1,1024,512]{2,1,0:T(8,128)(2,1)S(1)}, bf16[1,1024,512]{2,1,0:T(8,128)(2,1)}, u32[]{:S(2)}) copy-start(bf16[1,1024,512]{2,1,0:T(8,128)(2,1)} %param.13) | copy-start | bytes 3145732
Sparse Core Ops, SparseCore 0:
  9.6 37.1 all-gather.9
  48.8 51.0 all-gather.5
  102.0 49.2 all-gather.7
  189.3 42.6 reduce-scatter.1
where the time goes:
time: 242 us; the launch traced here: 241 us
  waiting for transfers between devices  79.7 us (33%)
  matrix products  71.7 us (30%)
  other arithmetic  39.6 us (16%)
  blocking collectives  22.2 us (9%)
  between operations  16.1 us (7%)
  local copies, waits for them, and re-layouts  11.6 us (5%)
    reduce_scatter x1, waiting for transfers between devices, on_device(): lax.psum_scatter(partial_value.astype(jnp.bfloat16), 'tp', scatter_dimens...  37.3 us
    all_gather x1, waiting for transfers between devices, on_device(): key_piece = lax.all_gather(prefix_k, 'req', axis=0, tiled=True)  32.2 us
    all_gather x1, blocking collectives, on_device(): number_piece = lax.all_gather(block_numbers, 'req', axis=0, tiled=True)  22.2 us
    dot_general x1, matrix products, on_device(): jnp.einsum('shd,khd->hsk', query_heads, compute_key_heads, preferred_elem...  17.8 us
    dot_general x1, matrix products, on_device(): jnp.einsum('hsk,khd->hsd', compute_weights.astype(jnp.bfloat16), compute_...  15.1 us
    reduce_sum x1, other arithmetic, on_device(): compute_new_sum = jnp.sum(compute_weights, axis=2)  14.3 us
    dot_general x2, matrix products, on_device(): jnp.einsum('shd,khd->hsk', query_block, key_heads, preferred_element_type...  12.3 us
    dot_general x1, matrix products, on_device(): jnp.einsum('sd,cdh->csh', normed, w_qkv, preferred_element_type=jnp.float32)  11.3 us
  transfers between devices with their start and end apart: 4, of which 4 were waited for; matrix products, arithmetic and copies ran while one was open for 34% of the time, Pallas kernels for 0%

commit v1 on v0

--- a/solution.py
+++ b/solution.py
@@ -5,6 +5,34 @@
 
 EPS = 1e-05
 NEGATIVE = -1e30
+
+
+def fill_pieces_all(buf, along_dim):
+    buf = jnp.moveaxis(buf, 0, along_dim)
+    a_next = buf.shape
+    return buf.reshape(
+        *a_next[:along_dim], a_next[along_dim] * a_next[along_dim + 1], *a_next[along_dim + 2 :]
+    )
+
+
+def compute_the_ports(field_in, comm_axis, which_dim):
+    many = lax.axis_size(comm_axis)
+    sides = [(p, (p + 1) % many) for p in range(many)]
+    v_now, piece_next = ([], [])
+    grid = [(h, d) for d, h in sides]
+    idx = 0
+    while idx < many - 1:
+        if idx % 2 == 0:
+            v_now.append(lax.ppermute(v_now[-1] if v_now else field_in, comm_axis, sides))
+        else:
+            piece_next.append(
+                lax.ppermute(piece_next[-1] if piece_next else field_in, comm_axis, grid)
+            )
+        idx += 1
+    tmp = jnp.stack([*v_now[::-1], field_in, *piece_next])
+    all_values = lax.axis_index(comm_axis) - len(v_now)
+    tmp = tmp[(jnp.arange(many) - all_values) % many]
+    return fill_pieces_all(tmp, which_dim)
 
 
 def on_device(
@@ -51,7 +79,7 @@
     prefix_total = half_count * block_tokens
     block_numbers = jnp.full((block_tokens,), block_of_device[0], jnp.int32)
     query_pos = (prefix_total + slot_ids).astype(jnp.float32)
-    key_piece = lax.all_gather(prefix_k, "req", axis=0, tiled=True)
+    key_piece = compute_the_ports(prefix_k, "req", 0)
     value_piece = lax.all_gather(prefix_v, "req", axis=0, tiled=True)
     number_piece = lax.all_gather(block_numbers, "req", axis=0, tiled=True)
     count = key_piece.shape[0]

time: 242 us -> 246 us (1.017)
  waiting for transfers between devices: 79.7 us -> 60.5 us
  starting transfers between devices: 0.16 us -> 14 us
  local copies, waits for them, and re-layouts: 11.6 us -> 23 us
    all_gather x1 -> x0, waiting for transfers between devices: 32.2 us -> none  [on_device(): key_piece = lax.all_gather(prefix_k, 'req', axis=0, tiled=True)]
    ppermute x0 -> x7, waiting for transfers between devices: none -> 19.5 us  [the longest x4 12.1 us: compute_the_ports(): lax.ppermute(v_now[-1] if v_now else field_in, comm_axis, sides)]
    ppermute x0 -> x7, starting transfers between devices: none -> 13.9 us  [the longest x3 7.83 us: compute_the_ports(): lax.ppermute(piece_next[-1] if piece_next else field_in, comm_axis, grid)]
    all_gather x1, waiting for transfers between devices: 6.73 us -> 0.02 us  [on_device(): value_piece = lax.all_gather(prefix_v, 'req', axis=0, tiled=True)]
    another operation x0 -> x2, local copies, waits for them, and re-layouts: none -> 4.7 us  [the longest x1 3.98 us: on_device(): compute_key_heads = key_piece.reshape(count, heads_dev, head_size)]
    gather x0 -> x1, local copies, waits for them, and re-layouts: none -> 3.63 us  [compute_the_ports(): tmp = tmp[(jnp.arange(many) - all_values) % many]]
    unnamed x49 -> x57, local copies, waits for them, and re-layouts: 8.48 us -> 11.5 us
    reduce_scatter x1, waiting for transfers between devices: 37.3 us -> 40.3 us  [on_device(): lax.psum_scatter(partial_value.astype(jnp.bfloat16), 'tp', scatter_dimens...]
  transfers between devices with their start and end apart: 4 -> 10, of which waited for: 4 -> 5; matrix products, arithmetic and copies ran while one was open for 34% -> 38% of each run, Pallas kernels for 0% -> 0%
where the time goes in v1:
time: 246 us
  matrix products  72.2 us (29%)
  waiting for transfers between devices  60.5 us (25%)
  other arithmetic  39.2 us (16%)
  local copies, waits for them, and re-layouts  23 us (9%)
  blocking collectives  20.7 us (8%)
  between operations  16.2 us (7%)
  starting transfers between devices  14 us (6%)
    reduce_scatter x1, waiting for transfers between devices, on_device(): lax.psum_scatter(partial_value.astype(jnp.bfloat16), 'tp', scatter_dimens...  40.3 us
    all_gather x1, blocking collectives, on_device(): number_piece = lax.all_gather(block_numbers, 'req', axis=0, tiled=True)  20.7 us
    dot_general x1, matrix products, on_device(): jnp.einsum('shd,khd->hsk', query_heads, compute_key_heads, preferred_elem...  18.4 us
    dot_general x1, matrix products, on_device(): jnp.einsum('hsk,khd->hsd', compute_weights.astype(jnp.bfloat16), compute_...  15.1 us
    reduce_sum x1, other arithmetic, on_device(): compute_new_sum = jnp.sum(compute_weights, axis=2)  14 us
    dot_general x2, matrix products, on_device(): jnp.einsum('shd,khd->hsk', query_block, key_heads, preferred_element_type...  12.5 us
    ppermute x4, waiting for transfers between devices, compute_the_ports(): lax.ppermute(v_now[-1] if v_now else field_in, comm_axis, sides)  12.1 us
    unnamed x57, local copies, waits for them, and re-layouts  11.5 us
  transfers between devices with their start and end apart: 10, of which 5 were waited for; matrix products, arithmetic and copies ran while one was open for 38% of the time, Pallas kernels for 0%

profile of v1, /device:TPU:0, one launch (start us, length us, event | category | flops | bytes accessed | tf_op | source)
XLA Modules:
  0.0 245.8 jit_solution(11849957231965866649)
XLA Ops:
  8.0 3.0 %collective-permute-start = (bf16[256,512]{1,0:T(8,128)(2,1)}, bf16[256,512]{1,0:T(8,128)(2,1)S(1)}, u32[]{:S(2)}, u32[]{:S(2)}) collective-permute-start(bf16[256,512]{1,0:T(8,128)(2,1)} %param.21), channel_id=1, source_target_pairs={{0,4},{4,8},{8,12},{12,16},{16,20},{20,24},{24,28},{28,0},{1,5},{5... | collective-permute-start | bytes 786440 | tf_op jit(solution)/shard_map/ppermute | solution.py:26
  11.0 3.1 %collective-permute-start.4 = (bf16[256,512]{1,0:T(8,128)(2,1)}, bf16[256,512]{1,0:T(8,128)(2,1)S(1)}, u32[]{:S(2)}, u32[]{:S(2)}) collective-permute-start(bf16[256,512]{1,0:T(8,128)(2,1)} %param.21), channel_id=1, source_target_pairs={{4,0},{8,4},{12,8},{16,12},{20,16},{24,20},{28,24},{0,28},{5,1},{9... | collective-permute-start | bytes 786440 | tf_op jit(solution)/shard_map/ppermute | solution.py:29
  14.1 1.8 copy.44
  16.6 20.7 %all-gather.1 = s32[8,1,256]{2,1,0:T(1,128)S(1)} all-gather(s32[1,1,256]{2,1,0:T(1,128)S(1)} %broadcast.232), channel_id=1, replica_groups=mesh['req'=8,'tp'=4] {'req'}, dimensions={0}, use_global_device_ids=true | all-gather | bytes 9216 | tf_op jit(solution)/shard_map/all_gather | solution.py:84
  37.3 3.8 %broadcast_subtract_fusion = f32[1024,2048]{1,0:T(8,128)} fusion(f32[2048]{0:T(1024)S(1)} %fusion.51, f32[1024]{0:T(1024)S(1)} %add_convert_fusion.1), kind=kLoop, calls=%fused_computation.29 | loop fusion | flops 2097152 | bytes 8400896 | tf_op jit(solution)/shard_map/sub | solution.py:99
  42.0 2.3 subtract_convert_fusion
  44.3 6.8 %collective-permute-done.1 = bf16[256,512]{1,0:T(8,128)(2,1)S(1)} collective-permute-done((bf16[256,512]{1,0:T(8,128)(2,1)S(1)}, bf16[256,512]{1,0:T(8,128)(2,1)S(1)}, u32[]{:S(2)}, u32[]{:S(2)}) %collective-permute-start.1) | collective-permute-done | bytes 262176 | tf_op jit(solution)/shard_map/ppermute | solution.py:26
  51.1 1.7 fusion.36
  52.8 4.7 %collective-permute-start.5 = (bf16[256,512]{1,0:T(8,128)(2,1)S(1)}, bf16[256,512]{1,0:T(8,128)(2,1)S(1)}, u32[]{:S(2)}, u32[]{:S(2)}) collective-permute-start(bf16[256,512]{1,0:T(8,128)(2,1)S(1)} %collective-permute-done.4), channel_id=1, source_target_pairs={{4,0},{8,4},{12,8},{16,12},{20,16},{24,20},{28,24},{0,28},{5,1},{9... | collective-permute-start | bytes 786440 | tf_op jit(solution)/shard_map/ppermute | solution.py:29
  57.5 5.4 %collective-permute-done.2 = bf16[256,512]{1,0:T(8,128)(2,1)S(1)} collective-permute-done((bf16[256,512]{1,0:T(8,128)(2,1)S(1)}, bf16[256,512]{1,0:T(8,128)(2,1)S(1)}, u32[]{:S(2)}, u32[]{:S(2)}) %collective-permute-start.2) | collective-permute-done | bytes 262176 | tf_op jit(solution)/shard_map/ppermute | solution.py:26
  62.9 3.0 %collective-permute-start.3 = (bf16[256,512]{1,0:T(8,128)(2,1)S(1)}, bf16[256,512]{1,0:T(8,128)(2,1)S(1)}, u32[]{:S(2)}, u32[]{:S(2)}) collective-permute-start(bf16[256,512]{1,0:T(8,128)(2,1)S(1)} %collective-permute-done.2), channel_id=1, source_target_pairs={{0,4},{4,8},{8,12},{12,16},{16,20},{20,24},{24,28},{28,0},{1,5},{5... | collective-permute-start | bytes 786440 | tf_op jit(solution)/shard_map/ppermute | solution.py:26
  66.5 6.1 %collective-permute-done.5 = bf16[256,512]{1,0:T(8,128)(2,1)S(1)} collective-permute-done((bf16[256,512]{1,0:T(8,128)(2,1)S(1)}, bf16[256,512]{1,0:T(8,128)(2,1)S(1)}, u32[]{:S(2)}, u32[]{:S(2)}) %collective-permute-start.5) | collective-permute-done | bytes 262176 | tf_op jit(solution)/shard_map/ppermute | solution.py:29
  79.7 3.6 %gather_fusion = bf16[8,256,512]{2,1,0:T(8,128)(2,1)} fusion(bf16[8,256,512]{2,1,0:T(8,128)(2,1)} %bitcast_dynamic-update-slice_fusion, s32[1024]{0:T(1024)S(1)} %pad_clamp_fusion), kind=kCustom, calls=%fused_computation | custom fusion | bytes 4194336 | tf_op jit(solution)/shard_map/gather | solution.py:34
  83.4 4.0 %reshape_reshape.3 = bf16[2048,4,128]{2,1,0:T(4,128)(2,1)} reshape(bf16[8,256,512]{2,1,0:T(8,128)(2,1)} %gather_fusion) | data formatting | bytes 4194304 | tf_op jit(solution)/shard_map/reshape;reshape | solution.py:90
  87.3 3.0 %convert_reduce_fusion = f32[1024]{0:T(1024)S(1)} fusion(bf16[1,1024,2048]{2,1,0:T(8,128)(2,1)} %all-gather.7.cloned.1.call-done), kind=kLoop, calls=%fused_computation.7 | loop fusion | flops 4193280 | bytes 4198400 | tf_op jit(solution)/shard_map/reduce_sum | solution.py:58
  90.3 3.4 %fusion.8 = f32[1024]{0:T(1024)S(1)} fusion(bf16[1,1024,2048]{2,1,0:T(8,128)(2,1)} %all-gather.7.cloned.1.call-done, f32[1024]{0:T(1024)S(1)} %broadcast_multiply_fusion), kind=kLoop, calls=%fused_computation.12 | loop fusion | flops 8387584 | bytes 4202496 | tf_op jit(solution)/shard_map/reduce_sum | solution.py:59
  93.8 11.1 %fusion.29 = bf16[3,1024,512]{1,2,0:T(8,128)(2,1)S(1)} fusion(f32[3,512]{1,0:T(4,128)S(1)} %copy-done.16, bf16[3,2048,512]{2,1,0:T(8,128)(2,1)} %param.16, bf16[1,1024,2048]{2,1,0:T(8,128)(2,1)S(1)} %copy-done.1, f32[2048]{0:T(1024)S(1)} %copy-done.17, f32[2048]{0:T(1024)S(1)} %copy-done.18, f32[1024]{0:T(1024)S(1)} %add_sqrt_fusion, ...), kind=kOutput, calls=%fused_computation.37 | convolution fusion | flops 6458179584 | bytes 13662208 | tf_op jit(solution)/shard_map/sd,cdh->csh/dot_general | solution.py:62
  104.9 2.1 broadcast_select_fusion
  108.1 18.4 %fusion.69 = (f32[4,1024]{1,0:T(4,128)S(1)}, f32[4,1024,2048]{2,1,0:T(8,128)}) fusion(f32[1024,2048]{1,0:T(8,128)} %broadcast_subtract_fusion, f32[4]{0:T(128)S(1)} %copy-done.15, bf16[1024,4,128]{0,2,1:T(8,128)(2,1)S(1)} %bitcast.78, bf16[2048,4,128]{2,1,0:T(4,128)(2,1)} %reshape_reshape.3, pred[2048]{0:T(1024)(128)(4,1)S(1)} %fusion.48), kind=kOutput, calls=%fused_computation.111 | convolution fusion | flops 2189422592 | bytes 45107216 | tf_op jit(solution)/shard_map/shd,khd->hsk/dot_general | solution.py:93
  126.5 4.7 %fusion.16 = (f32[4,512]{1,0:T(4,128)S(1)}, f32[4,512,1024]{2,1,0:T(8,128)S(1)}) fusion(f32[512,1024]{1,0:T(8,128)} %get-tuple-element.35, f32[4]{0:T(128)S(1)} %copy-done.15, pred[512,1024]{1,0:T(8,128)(4,1)} %get-tuple-element.28, bf16[512,4,128]{0,2,1:T(8,128)(2,1)} %bitcast.85, bf16[1024,4,128]{0,2,1:T(8,128)(2,1)} %bitcast.81), kind=kOutput, calls=%fused_computation.25 | convolution fusion | flops 547354624 | bytes 12591120 | tf_op jit(solution)/shard_map/shd,khd->hsk/dot_general | solution.py:122
  131.3 7.8 %fusion.12 = (f32[4,512]{1,0:T(4,128)S(1)}, f32[4,512]{1,0:T(4,128)S(1)}, f32[4,512,1024]{2,1,0:T(8,128)}) fusion(f32[4,512,1024]{2,1,0:T(8,128)S(1)} %get-tuple-element.30, f32[4,512]{1,0:T(4,128)S(1)} %slice_maximum_fusion.1, f32[512,1024]{1,0:T(8,128)S(1)} %copy-done.7, f32[4]{0:T(128)S(1)} %copy-done.15, pred[512,1024]{1,0:T(8,128)(4,1)S(1)} %copy-done.11, ...), kind=kOutput, calls=%fused_computation.20 | convolution fusion | flops 562032640 | bytes 23617552 | tf_op jit(solution)/shard_map/shd,khd->hsk/dot_general | solution.py:122
  139.1 14.0 %fusion = f32[4,1024]{1,0:T(4,128)S(1)} fusion(f32[4,1024,2048]{2,1,0:T(8,128)} %get-tuple-element.32, f32[4,1024]{1,0:T(4,128)S(1)} %broadcast_maximum_fusion, pred[2048]{0:T(1024)(128)(4,1)S(1)} %fusion.48), kind=kLoop, calls=%fused_computation.3 | loop fusion | flops 25161728 | bytes 33589248 | tf_op jit(solution)/shard_map/reduce_sum | solution.py:106
  153.2 15.1 %fusion.2 = f32[4,1024,128]{2,1,0:T(8,128)} fusion(bf16[2048,4,128]{0,2,1:T(8,128)(2,1)} %bitcast.88, f32[4,1024,2048]{2,1,0:T(8,128)} %get-tuple-element.32, f32[4,1024]{1,0:T(4,128)S(1)} %broadcast_maximum_fusion, pred[2048]{0:T(1024)(128)(4,1)S(1)} %fusion.48), kind=kOutput, calls=%fused_computation.5 | convolution fusion | flops 2172649472 | bytes 37767168 | tf_op jit(solution)/shard_map/hsk,khd->hsd/dot_general | solution.py:107
  168.3 6.0 %fusion.14 = f32[4,512]{1,0:T(4,128)S(1)} fusion(f32[4,512,1024]{2,1,0:T(8,128)} %get-tuple-element.33, f32[4,512]{1,0:T(4,128)S(1)} %slice_maximum_fusion, f32[512,1024]{1,0:T(8,128)S(1)} %copy-done.4, f32[4]{0:T(128)S(1)} %copy-done.15, pred[512,1024]{1,0:T(8,128)(4,1)S(1)} %copy-done.6), kind=kLoop, calls=%fused_computation.22 | loop fusion | flops 14678016 | bytes 11026448 | tf_op jit(solution)/shard_map/reduce_sum | solution.py:136
  174.4 5.8 %divide_convert_fusion = bf16[4,512,128]{2,1,0:T(8,128)(2,1)S(1)} fusion(bf16[1024,4,128]{0,2,1:T(8,128)(2,1)S(1)} %bitcast.79, f32[4,512,1024]{2,1,0:T(8,128)S(1)} %copy-done.2, f32[4,512]{1,0:T(4,128)S(1)} %slice_maximum_fusion, f32[512,1024]{1,0:T(8,128)S(1)} %copy-done.4, f32[4]{0:T(128)S(1)} %copy-done.15, pred[512,1024]{1,0:T(8,128)(4,1)S(1)} %copy-done.6, ...), kind=kOutput, calls=%fused_computation.54 | convolution fusion | flops 552599552 | bytes 13656080 | tf_op jit(solution)/shard_map/hsk,khd->hsd/dot_general | solution.py:137
  180.3 3.8 %divide_convert_fusion.1 = bf16[4,512,128]{2,1,0:T(8,128)(2,1)S(1)} fusion(bf16[1024,4,128]{0,2,1:T(8,128)(2,1)S(1)} %bitcast.80, f32[4,512,1024]{2,1,0:T(8,128)S(1)} %bitcast.90, f32[4,512]{1,0:T(4,128)S(1)} %slice_maximum_fusion.1, f32[512,1024]{1,0:T(8,128)S(1)} %copy-done.8, f32[4]{0:T(128)S(1)} %copy-done.15, pred[512,1024]{1,0:T(8,128)(4,1)S(1)} %copy-done.12, ...), kind=kOutput, calls=%fused_computation.55 | convolution fusion | flops 552599552 | bytes 13656080 | tf_op jit(solution)/shard_map/hsk,khd->hsd/dot_general | solution.py:137
  184.1 1.3 copy.52
  185.4 5.6 %convolution_convert_fusion = bf16[1024,2048]{1,0:T(8,128)(2,1)} fusion(bf16[1024,512]{0,1:T(8,128)(2,1)} %bitcast.83, bf16[512,2048]{1,0:T(8,128)(2,1)S(1)} %copy-done), kind=kOutput, calls=%fused_computation.36 | convolution fusion | flops 2149580800 | bytes 7340032 | tf_op jit(solution)/shard_map/dot_general | solution.py:149
  191.9 2.3 copy.53
  194.1 2.3 copy.54
  196.4 40.3 %reduce-scatter.2.cloned.1.call-done = bf16[1024,512]{1,0:T(8,128)(2,1)} async-done(((bf16[1024,2048]{1,0:T(8,128)(2,1)}), bf16[1024,512]{1,0:T(8,128)(2,1)}) %reduce-scatter.2.cloned.1.call-update) | async-done | bytes 1048592 | tf_op jit(solution)/shard_map/reduce_scatter | solution.py:150
  236.7 2.6 %fusion.43 = bf16[1,1024,512]{2,1,0:T(8,128)(2,1)} fusion(bf16[1024,512]{1,0:T(8,128)(2,1)} %reduce-scatter.2.cloned.1.call-done, bf16[1,1024,512]{2,1,0:T(8,128)(2,1)S(1)} %copy-done.5, f32[512]{0:T(512)S(1)} %dynamic_slice.3, pred[1024]{0:T(1024)(128)(4,1)S(1)} %iota_compare_fusion.2), kind=kLoop, calls=%fused_computation.50 | loop fusion | flops 3145728 | bytes 3148800 | tf_op jit(solution)/shard_map/broadcast_in_dim | solution.py:156
  (90 shorter events, 10.1 us)
Async XLA Ops:
  7.2 178.3 %copy-start = (bf16[512,2048]{1,0:T(8,128)(2,1)S(1)}, bf16[512,2048]{1,0:T(8,128)(2,1)}, u32[]{:S(2)}) copy-start(bf16[512,2048]{1,0:T(8,128)(2,1)} %param.18) | copy-start | bytes 6291460
  7.2 80.2 %all-gather.7.cloned.1.call-start = ((), (), s32[]{:S(2)}) async-start(), calls=%async_computation.3 | async-start | bytes 5242880 | tf_op jit(solution)/shard_map/all_gather | solution.py:56
  7.9 67.6 %copy-start.14 = (bf16[256,512]{1,0:T(8,128)(2,1)S(1)}, bf16[256,512]{1,0:T(8,128)(2,1)}, u32[]{:S(2)}) copy-start(bf16[256,512]{1,0:T(8,128)(2,1)} %param.21) | copy-start | bytes 786436
  7.9 145.2 %all-gather.5.cloned.1.call-start = ((), (), s32[]{:S(2)}) async-start(), calls=%async_computation.1 | async-start | bytes 2359296 | tf_op jit(solution)/shard_map/all_gather | solution.py:83
  8.0 33.9 %collective-permute-start = (bf16[256,512]{1,0:T(8,128)(2,1)}, bf16[256,512]{1,0:T(8,128)(2,1)S(1)}, u32[]{:S(2)}, u32[]{:S(2)}) collective-permute-start(bf16[256,512]{1,0:T(8,128)(2,1)} %param.21), channel_id=1, source_target_pairs={{0,4},{4,8},{8,12},{12,16},{16,20},{20,24},{24,28},{28,0},{1,5},{5... | collective-permute-start | bytes 786440 | tf_op jit(solution)/shard_map/ppermute | solution.py:26
  11.0 41.8 %collective-permute-start.4 = (bf16[256,512]{1,0:T(8,128)(2,1)}, bf16[256,512]{1,0:T(8,128)(2,1)S(1)}, u32[]{:S(2)}, u32[]{:S(2)}) collective-permute-start(bf16[256,512]{1,0:T(8,128)(2,1)} %param.21), channel_id=1, source_target_pairs={{4,0},{8,4},{12,8},{16,12},{20,16},{24,20},{28,24},{0,28},{5,1},{9... | collective-permute-start | bytes 786440 | tf_op jit(solution)/shard_map/ppermute | solution.py:29
  15.9 220.8 %reduce-scatter.2.cloned.1.call-start = ((), (), s32[]{:S(2)}) async-start(), calls=%async_computation.2 | async-start | bytes 5242880 | tf_op jit(solution)/shard_map/reduce_scatter | solution.py:150
  41.9 9.2 %collective-permute-start.1 = (bf16[256,512]{1,0:T(8,128)(2,1)S(1)}, bf16[256,512]{1,0:T(8,128)(2,1)S(1)}, u32[]{:S(2)}, u32[]{:S(2)}) collective-permute-start(bf16[256,512]{1,0:T(8,128)(2,1)S(1)} %collective-permute-done), channel_id=1, source_target_pairs={{0,4},{4,8},{8,12},{12,16},{16,20},{20,24},{24,28},{28,0},{1,5},{5... | collective-permute-start | bytes 786440 | tf_op jit(solution)/shard_map/ppermute | solution.py:26
  51.1 11.8 %collective-permute-start.2 = (bf16[256,512]{1,0:T(8,128)(2,1)S(1)}, bf16[256,512]{1,0:T(8,128)(2,1)S(1)}, u32[]{:S(2)}, u32[]{:S(2)}) collective-permute-start(bf16[256,512]{1,0:T(8,128)(2,1)S(1)} %collective-permute-done.1), channel_id=1, source_target_pairs={{0,4},{4,8},{8,12},{12,16},{16,20},{20,24},{24,28},{28,0},{1,5},{5... | collective-permute-start | bytes 786440 | tf_op jit(solution)/shard_map/ppermute | solution.py:26
  52.8 19.8 %collective-permute-start.5 = (bf16[256,512]{1,0:T(8,128)(2,1)S(1)}, bf16[256,512]{1,0:T(8,128)(2,1)S(1)}, u32[]{:S(2)}, u32[]{:S(2)}) collective-permute-start(bf16[256,512]{1,0:T(8,128)(2,1)S(1)} %collective-permute-done.4), channel_id=1, source_target_pairs={{4,0},{8,4},{12,8},{16,12},{20,16},{24,20},{28,24},{0,28},{5,1},{9... | collective-permute-start | bytes 786440 | tf_op jit(solution)/shard_map/ppermute | solution.py:29
  62.9 9.8 %collective-permute-start.3 = (bf16[256,512]{1,0:T(8,128)(2,1)S(1)}, bf16[256,512]{1,0:T(8,128)(2,1)S(1)}, u32[]{:S(2)}, u32[]{:S(2)}) collective-permute-start(bf16[256,512]{1,0:T(8,128)(2,1)S(1)} %collective-permute-done.2), channel_id=1, source_target_pairs={{0,4},{4,8},{8,12},{12,16},{16,20},{20,24},{24,28},{28,0},{1,5},{5... | collective-permute-start | bytes 786440 | tf_op jit(solution)/shard_map/ppermute | solution.py:26
  72.6 6.4 %collective-permute-start.6 = (bf16[256,512]{1,0:T(8,128)(2,1)S(1)}, bf16[256,512]{1,0:T(8,128)(2,1)S(1)}, u32[]{:S(2)}, u32[]{:S(2)}) collective-permute-start(bf16[256,512]{1,0:T(8,128)(2,1)S(1)} %collective-permute-done.5), channel_id=1, source_target_pairs={{4,0},{8,4},{12,8},{16,12},{20,16},{24,20},{28,24},{0,28},{5,1},{9... | collective-permute-start | bytes 786440 | tf_op jit(solution)/shard_map/ppermute | solution.py:29
  79.7 14.0 %copy-start.16 = (f32[3,512]{1,0:T(4,128)S(1)}, f32[3,512]{1,0:T(4,128)}, u32[]{:S(2)}) copy-start(f32[3,512]{1,0:T(4,128)} %param.17) | copy-start | bytes 18436
  79.7 14.0 %copy-start.17 = (f32[2048]{0:T(1024)S(1)}, f32[2048]{0:T(1024)}, u32[]{:S(2)}) copy-start(f32[2048]{0:T(1024)} %param.15) | copy-start | bytes 24580
  79.7 14.0 %copy-start.18 = (f32[2048]{0:T(1024)S(1)}, f32[2048]{0:T(1024)}, u32[]{:S(2)}) copy-start(f32[2048]{0:T(1024)} %param.14) | copy-start | bytes 24580
  87.3 6.4 %copy-start.1 = (bf16[1,1024,2048]{2,1,0:T(8,128)(2,1)S(1)}, bf16[1,1024,2048]{2,1,0:T(8,128)(2,1)}, u32[]{:S(2)}) copy-start(bf16[1,1024,2048]{2,1,0:T(8,128)(2,1)} %all-gather.7.cloned.1.call-done) | copy-start | bytes 12582916
  126.4 4.8 %copy-start.3 = (f32[512,1024]{1,0:T(8,128)S(1)}, f32[512,1024]{1,0:T(8,128)}, u32[]{:S(2)}) copy-start(f32[512,1024]{1,0:T(8,128)} %get-tuple-element.34) | copy-start | bytes 6291460
  126.4 4.8 %copy-start.6 = (pred[512,1024]{1,0:T(8,128)(4,1)S(1)}, pred[512,1024]{1,0:T(8,128)(4,1)}, u32[]{:S(2)}) copy-start(pred[512,1024]{1,0:T(8,128)(4,1)} %get-tuple-element.27) | copy-start | bytes 1572868
  126.4 4.8 %copy-start.7 = (f32[512,1024]{1,0:T(8,128)S(1)}, f32[512,1024]{1,0:T(8,128)}, u32[]{:S(2)}) copy-start(f32[512,1024]{1,0:T(8,128)} %get-tuple-element.35) | copy-start | bytes 6291460
  126.5 4.8 %copy-start.10 = (bf16[1,1024,512]{1,2,0:T(8,128)(2,1)S(1)}, bf16[1,1024,512]{1,2,0:T(8,128)(2,1)}, u32[]{:S(2)}) copy-start(bf16[1,1024,512]{1,2,0:T(8,128)(2,1)} %get-tuple-element.21) | copy-start | bytes 3145732
  126.5 4.8 %copy-start.11 = (pred[512,1024]{1,0:T(8,128)(4,1)S(1)}, pred[512,1024]{1,0:T(8,128)(4,1)}, u32[]{:S(2)}) copy-start(pred[512,1024]{1,0:T(8,128)(4,1)} %get-tuple-element.28) | copy-start | bytes 1572868
  126.5 4.8 %copy-start.13 = (bf16[1,512,512]{1,2,0:T(8,128)(2,1)S(1)}, bf16[1,512,512]{1,2,0:T(8,128)(2,1)}, u32[]{:S(2)}) copy-start(bf16[1,512,512]{1,2,0:T(8,128)(2,1)} %get-tuple-element.24) | copy-start | bytes 1572868
  131.2 7.9 %copy-start.19 = (f32[4,512,1024]{2,1,0:T(8,128)}, f32[4,512,1024]{2,1,0:T(8,128)S(1)}, u32[]{:S(2)}) copy-start(f32[4,512,1024]{2,1,0:T(8,128)S(1)} %get-tuple-element.30) | copy-start | bytes 25165828
  153.2 15.1 %copy-start.4 = (f32[512,1024]{1,0:T(8,128)S(1)}, f32[512,1024]{1,0:T(8,128)}, u32[]{:S(2)}) copy-start(f32[512,1024]{1,0:T(8,128)} %get-tuple-element.34) | copy-start | bytes 6291460
  168.2 6.1 %copy-start.2 = (f32[4,512,1024]{2,1,0:T(8,128)S(1)}, f32[4,512,1024]{2,1,0:T(8,128)}, u32[]{:S(2)}) copy-start(f32[4,512,1024]{2,1,0:T(8,128)} %get-tuple-element.33) | copy-start | bytes 25165828
  168.2 6.1 %copy-start.9 = (bf16[1,1024,512]{1,2,0:T(8,128)(2,1)S(1)}, bf16[1,1024,512]{1,2,0:T(8,128)(2,1)}, u32[]{:S(2)}) copy-start(bf16[1,1024,512]{1,2,0:T(8,128)(2,1)} %get-tuple-element.20) | copy-start | bytes 3145732
  168.2 12.0 %slice-start = ((s8[8388608]{0:T(1024)(128)(4,1)}), s8[4194304]{0:T(1024)(128)(4,1)S(1)}, s32[]{:S(2)}) async-start(s8[8388608]{0:T(1024)(128)(4,1)} %bitcast.89), calls=%async_computation.4 | async-start | bytes 8388608
  174.3 5.9 %copy-start.8 = (f32[512,1024]{1,0:T(8,128)S(1)}, f32[512,1024]{1,0:T(8,128)}, u32[]{:S(2)}) copy-start(f32[512,1024]{1,0:T(8,128)} %get-tuple-element.35) | copy-start | bytes 6291460
  174.3 5.9 %copy-start.12 = (pred[512,1024]{1,0:T(8,128)(4,1)S(1)}, pred[512,1024]{1,0:T(8,128)(4,1)}, u32[]{:S(2)}) copy-start(pred[512,1024]{1,0:T(8,128)(4,1)} %get-tuple-element.28) | copy-start | bytes 1572868
  174.3 5.9 %slice-start.1 = ((s8[8388608]{0:T(1024)(128)(4,1)}), s8[4194304]{0:T(1024)(128)(4,1)S(1)}, s32[]{:S(2)}) async-start(s8[8388608]{0:T(1024)(128)(4,1)} %bitcast.89), calls=%async_computation.5 | async-start | bytes 8388608
  174.4 5.9 %copy-start.20 = (f32[4,1024,128]{2,1,0:T(8,128)S(1)}, f32[4,1024,128]{2,1,0:T(8,128)}, u32[]{:S(2)}) copy-start(f32[4,1024,128]{2,1,0:T(8,128)} %fusion.2) | copy-start | bytes 6291460
  185.4 51.3 %copy-start.5 = (bf16[1,1024,512]{2,1,0:T(8,128)(2,1)S(1)}, bf16[1,1024,512]{2,1,0:T(8,128)(2,1)}, u32[]{:S(2)}) copy-start(bf16[1,1024,512]{2,1,0:T(8,128)(2,1)} %param.13) | copy-start | bytes 3145732
  (1 other events, 3.2 us)
Sparse Core Ops, SparseCore 0:
  9.6 37.1 all-gather.6
  48.8 59.1 all-gather.4
  191.2 45.4 reduce-scatter.1
